TPU v7x, 32 devices: a whole 2x2x4 slice. The times are simulated.
32 devices in a mesh: slab: 8 (over z, y), rays: 4 (over x, core).
Axes of the slice: x: 2, y: 2, z: 4, core: 2. Of those that a mesh axis runs over, the one named last changes fastest.
Arguments:
- geometry: float32 [6, 4, 128], P(None, 'rays'), may hold values from -1 to 1
- entry: int32 [8, 4, 128], P('slab', 'rays'), may hold values from 0 to 63
- counts: int32 [8, 4, 128], P('slab', 'rays'), may hold values from 0 to 8
- targets: float32 [3, 4, 128], P(None, 'rays', 'slab'), may hold values from 0 to 1
- w_in: float32 [8, 256, 256], P('slab'), may hold values from -0.375 to 0.375
- w_mid: float32 [8, 2, 256, 256], P('slab'), may hold values from -0.375 to 0.375
- w_out: float32 [8, 4, 256], P('slab'), may hold values from -0.375 to 0.375
- b_hid: float32 [8, 3, 256], P('slab'), may hold values from -3 to 3
- b_out: float32 [8, 4], P('slab'), may hold values from -3 to 3
- freqs: float32 [8, 3, 128], P('slab'), may hold values from -3 to 3
Outputs:
- pixels: float32 [3, 4, 128], P(None, 'rays', 'slab')
- grad_in: float32 [8, 256, 256], P('slab')
- grad_mid: float32 [8, 2, 256, 256], P('slab')
- grad_out: float32 [8, 4, 256], P('slab')
- grad_hid: float32 [8, 3, 256], P('slab')
- grad_bout: float32 [8, 4], P('slab')
Inputs may be any that keep to these rules, and one draw needn't show every extreme that they name: `entry`: the index of a ray's first sample in a slab. `counts`: how many of the 8 slots of a ray lie inside a slab; 0 where the ray misses it.
All inputs are finite; a program needn't handle non-finite values.
Results may differ from a plain program's by a relative error of at most 0.0003.
Values sent between devices are 32-bit elements; how exact they have to be, the bound alone decides.
A program may use at most 128 MiB of HBM per device.

v0:
```python
import math
import jax
import jax.numpy as jnp
from jax import lax
from jax.sharding import PartitionSpec as P

MID = 2
SAMP = 8
RAY_DEV = 16
HIGH = lax.Precision.HIGHEST


def features(freqs, geometry, entry):
    width = geometry.shape[1]
    slots = jnp.arange(SAMP, dtype=jnp.int32)[:, None]
    times = 0.25 * (entry.astype(jnp.float32)[None, :] + slots.astype(jnp.float32) + 0.5)
    places = geometry[0:3, None, :] + times[None] * geometry[3:6, None, :]
    places = places.reshape(3, SAMP * width)
    phase = jnp.einsum("dk,dn->nk", freqs, places, precision=HIGH)
    return jnp.concatenate([jnp.sin(phase), jnp.cos(phase)], axis=1)


def hidden_layer(hidden, weight, bias):
    return jax.nn.softplus(jnp.dot(hidden, weight, precision=HIGH) + bias)


def head(hidden, w_out, b_out, counts, delta):
    width = counts.shape[0]
    slots = jnp.arange(SAMP, dtype=jnp.int32)[:, None]
    result = jnp.einsum("ch,nh->cn", w_out, hidden, precision=HIGH) + b_out[:, None]
    sigma = jax.nn.softplus(result[0]).reshape(SAMP, width)
    colors = jax.nn.sigmoid(result[1:]).reshape(3, SAMP, width)
    alive = slots < counts[None, :]
    depth = jnp.where(alive, sigma * delta, jnp.float32(0.0))
    before = jnp.cumsum(depth, axis=0) - depth
    weights = jnp.exp(-before) * (1.0 - jnp.exp(-depth))
    color = jnp.sum(weights[None] * colors, axis=1)
    logtrans = -jnp.sum(depth, axis=0)
    return jnp.concatenate([color, logtrans[None]], axis=0)


def segment(params, encoded, counts, delta):
    hidden = hidden_layer(encoded, params[0], params[3][0])
    for layer in range(MID):
        hidden = hidden_layer(hidden, params[1][layer], params[3][layer + 1])
    return head(hidden, params[2], params[4], counts, delta)


def composite(segments, targets, factor):
    logtrans = segments[3]
    before = jnp.cumsum(logtrans, axis=0) - logtrans
    shade = jnp.exp(before)
    pixels = jnp.sum(shade[None] * segments[:3], axis=1) + jnp.exp(jnp.sum(logtrans, axis=0))[None]
    loss = factor * jnp.sum((pixels - targets) ** 2)
    return (loss, pixels)


def shards(geometry, entry, counts, targets, w_in, w_mid, w_out, b_hid, b_out, freqs):
    slabs = lax.axis_size("slab")
    delta = 3.0 / (SAMP * slabs)
    factor = 1.0 / math.sqrt(3.0 * lax.axis_size("rays") * slabs * RAY_DEV)
    local_geometry = geometry[:, 0, :]
    local_entry = entry[0, 0]
    local_counts = counts[0, 0]
    local_targets = targets[:, 0, :]
    params = (w_in[0], w_mid[0], w_out[0], b_hid[0], b_out[0])
    encoded = features(freqs[0], local_geometry, local_entry)
    seg, pull_all = jax.vjp(lambda p: segment(p, encoded, local_counts, delta), params)
    owned = lax.all_to_all(seg[:, None, :], "slab", split_axis=2, concat_axis=1, tiled=True)
    loss, pullback, pixels = jax.vjp(
        lambda s: composite(s, local_targets, factor), owned, has_aux=True
    )
    owned_adjoint = pullback(jnp.ones((), jnp.float32))[0]
    adjoint = lax.all_to_all(owned_adjoint, "slab", split_axis=1, concat_axis=2, tiled=True)[
        :, 0, :
    ]
    grads = pull_all(adjoint)[0]
    grad_in, grad_mid, grad_out, grad_hid, grad_bout = lax.psum(
        (grads[0], grads[1], grads[2], grads[3], grads[4]), "rays"
    )
    return (
        pixels[:, None, :],
        grad_in[None],
        grad_mid[None],
        grad_out[None],
        grad_hid[None],
        grad_bout[None],
    )


def solution(mesh):
    in_specs = (
        P(None, "rays", None),
        P("slab", "rays", None),
        P("slab", "rays", None),
        P(None, "rays", "slab"),
        P("slab", None, None),
        P("slab", None, None, None),
        P("slab", None, None),
        P("slab", None, None),
        P("slab", None),
        P("slab", None, None),
    )
    out_specs = (
        P(None, "rays", "slab"),
        P("slab", None, None),
        P("slab", None, None, None),
        P("slab", None, None),
        P("slab", None, None),
        P("slab", None),
    )
    return jax.shard_map(shards, mesh=mesh, in_specs=in_specs, out_specs=out_specs, check_vma=False)
```

profile of v0, /device:TPU:0, one launch (start us, length us, event | category | flops | bytes accessed | tf_op | source)
XLA Modules:
  0.0 106.8 jit_solution(6340818017745772977)
XLA Ops:
  7.2 0.0 copy-start
  7.2 0.7 copy-done.9
  7.9 0.0 copy-done.2
  7.9 0.7 copy-done.3
  8.6 0.1 add_multiply_fusion
  8.7 0.7 copy-done.4
  9.4 5.2 %fusion.69 = (f32[1024,128]{0,1:T(8,128)S(1)}, f32[1024,128]{0,1:T(8,128)S(1)}) fusion(f32[1,3,128]{2,0,1:T(1,128)S(1)} %copy-done.4, f32[1,3,8,128]{3,2,1,0:T(8,128)S(1)} %add_bitcast_fusion.1), kind=kOutput, calls=%fused_computation.129 | convolution fusion | flops 4718592 | bytes 1062400 | tf_op jit(solution)/shard_map/dk,dn->nk/dot_general | solution.py:19
  14.6 1.8 %convolution_add_fusion.2 = f32[1024,256]{1,0:T(8,128)S(1)} fusion(f32[1024,128]{0,1:T(8,128)S(1)} %get-tuple-element.64, f32[1024,128]{0,1:T(8,128)S(1)} %get-tuple-element.63, f32[256]{0:T(256)S(1)} %bitcast.147, f32[1,256,256]{2,1,0:T(8,128)S(1)} %copy-done), kind=kOutput, calls=%fused_computation.14 | convolution fusion | flops 805830656 | bytes 2360320 | tf_op jit(solution)/shard_map/jvp()/dot_general | solution.py:24
  16.4 1.4 %convolution_add_fusion.1 = f32[1024,256]{1,0:T(8,128)S(1)} fusion(f32[1024,256]{1,0:T(8,128)S(1)} %convolution_add_fusion.2, f32[256]{0:T(256)S(1)} %bitcast.156, f32[1,2,256,256]{3,2,1,0:T(8,128)S(1)} %copy-done.7), kind=kOutput, calls=%fused_computation.13 | convolution fusion | flops 807141376 | bytes 2360320 | tf_op jit(solution)/shard_map/jvp()/dot_general | solution.py:24
  17.9 0.0 copy-start.8
  17.9 1.5 %convolution_add_fusion = f32[1024,256]{1,0:T(8,128)S(1)} fusion(f32[1024,256]{1,0:T(8,128)S(1)} %convolution_add_fusion.1, f32[256]{0:T(256)S(1)} %bitcast.155, f32[1,2,256,256]{3,2,1,0:T(8,128)S(1)} %copy-done.7), kind=kOutput, calls=%fused_computation.12 | convolution fusion | flops 807141376 | bytes 2360320 | tf_op jit(solution)/shard_map/jvp()/dot_general | solution.py:24
  19.4 0.7 copy-done.10
  20.0 1.5 %fusion = f32[4,1024]{1,0:T(4,128)S(1)} fusion(f32[1024,256]{1,0:T(8,128)S(1)} %convolution_add_fusion, f32[4]{0:T(128)S(1)} %bitcast.157, f32[1,4,256]{2,1,0:T(4,128)S(1)} %copy-done.8), kind=kOutput, calls=%fused_computation.19 | convolution fusion | flops 14159872 | bytes 1069072 | tf_op jit(solution)/shard_map/jvp(ch,nh->cn)/dot_general | solution.py:30
  21.5 0.0 copy-done.13
  21.6 0.6 copy-done.5
  22.4 0.8 copy.29
  23.1 7.3 %all-to-all-start = ((f32[4,1,128]{0,1,2:T(1,128)}), f32[4,1,128]{0,1,2:T(1,128)S(1)}, u32[]{:S(2)}, u32[]{:S(2)}) async-start(f32[4,1,128]{0,1,2:T(1,128)} %bitcast.13), calls=%async_computation | async-start | bytes 131072 | tf_op jit(solution)/shard_map/all_to_all | solution.py:69
  30.5 6.9 %all-to-all-done = f32[4,1,128]{0,1,2:T(1,128)S(1)} async-done(((f32[4,1,128]{0,1,2:T(1,128)}), f32[4,1,128]{0,1,2:T(1,128)S(1)}, u32[]{:S(2)}, u32[]{:S(2)}) %all-to-all-start) | async-done | bytes 2080 | tf_op jit(solution)/shard_map/all_to_all | solution.py:69
  37.3 1.8 %slice_reduce_fusion = f32[128]{0:T(128)S(1)} fusion(f32[4,1,128]{0,1,2:T(1,128)S(1)} %all-to-all-done), kind=kLoop, calls=%fused_computation.44 | loop fusion | bytes 1024 | tf_op jit(solution)/shard_map/jvp()/slice | solution.py:50
  39.2 0.1 squeeze.39
  39.3 0.1 squeeze.42
  39.3 0.1 copy.38
  39.5 0.1 slice.59
  39.6 0.7 copy-done.6
  40.3 0.1 broadcast_in_dim.73
  40.4 0.1 reshape.387
  40.6 0.6 copy.31
  41.2 3.3 %all-to-all-start.1 = ((f32[4,8,16]{2,0,1:T(4,128)}), f32[4,8,16]{2,0,1:T(4,128)S(1)}, u32[]{:S(2)}, u32[]{:S(2)}) async-start(f32[4,8,16]{2,0,1:T(4,128)} %copy.31), calls=%async_computation.1 | async-start | bytes 32768 | tf_op jit(solution)/shard_map/all_to_all | solution.py:74
  44.5 0.2 all-reduce.13.cloned.1.call-start
  44.8 6.3 %all-to-all-done.1 = f32[4,8,16]{2,0,1:T(4,128)S(1)} async-done(((f32[4,8,16]{2,0,1:T(4,128)}), f32[4,8,16]{2,0,1:T(4,128)S(1)}, u32[]{:S(2)}, u32[]{:S(2)}) %all-to-all-start.1) | async-done | bytes 2080 | tf_op jit(solution)/shard_map/all_to_all | solution.py:74
  51.1 0.1 neg.109
  51.2 0.1 split.9
  51.3 0.1 fusion.36
  51.4 3.0 %fusion.75 = (f32[256]{0:T(256)S(1)}, f32[1024,256]{1,0:T(8,128)S(1)}) fusion(f32[1024,256]{1,0:T(8,128)} %copy-done.13, f32[1,4,256]{2,1,0:T(4,128)S(1)} %copy-done.8, f32[1,1024]{1,0:T(1,128)S(1)} %fusion.36, f32[3,1024]{1,0:T(4,128)S(1)} %get-tuple-element.65), kind=kOutput, calls=%fused_computation.135 | convolution fusion | flops 15994624 | bytes 2118656 | tf_op jit(solution)/shard_map/transpose(jvp(ch,nh->cn))/dot_general | solution.py:30
  54.5 2.3 %convolution_bitcast_fusion.1 = f32[1,256,256]{2,1,0:T(8,128)S(1)} fusion(f32[1024,256]{1,0:T(8,128)S(1)} %get-tuple-element.80, f32[1024,256]{1,0:T(8,128)S(1)} %copy-done.12), kind=kOutput, calls=%fused_computation.16 | convolution fusion | flops 806879232 | bytes 2359296 | tf_op jit(solution)/shard_map/transpose(jvp())/dot_general | solution.py:24
  56.7 1.7 %fusion.74 = (f32[256]{0:T(256)S(1)}, f32[1024,256]{1,0:T(8,128)S(1)}) fusion(f32[1024,256]{1,0:T(8,128)S(1)} %copy-done.12, f32[1024,256]{1,0:T(8,128)S(1)} %get-tuple-element.80, f32[1,2,256,256]{3,2,1,0:T(8,128)S(1)} %copy-done.7), kind=kOutput, calls=%fused_computation.134 | convolution fusion | flops 808713984 | bytes 3408896 | tf_op jit(solution)/shard_map/transpose(jvp())/dot_general | solution.py:24
  58.4 2.3 %convolution_bitcast_fusion = f32[1,256,256]{2,1,0:T(8,128)S(1)} fusion(f32[1024,256]{1,0:T(8,128)S(1)} %get-tuple-element.78, f32[1024,256]{1,0:T(8,128)S(1)} %convolution_add_fusion.2), kind=kOutput, calls=%fused_computation.15 | convolution fusion | flops 806879232 | bytes 2359296 | tf_op jit(solution)/shard_map/transpose(jvp())/dot_general | solution.py:24
  60.7 1.7 %fusion.73 = (f32[256]{0:T(256)S(1)}, f32[1024,256]{1,0:T(8,128)S(1)}) fusion(f32[1024,256]{1,0:T(8,128)S(1)} %convolution_add_fusion.2, f32[1024,256]{1,0:T(8,128)S(1)} %get-tuple-element.78, f32[1,2,256,256]{3,2,1,0:T(8,128)S(1)} %copy-done.7), kind=kOutput, calls=%fused_computation.133 | convolution fusion | flops 808713984 | bytes 3408896 | tf_op jit(solution)/shard_map/transpose(jvp())/dot_general | solution.py:24
  62.4 1.7 %convolution_bitcast_fusion.2 = f32[1,256,256]{2,1,0:T(8,128)} fusion(f32[1024,256]{1,0:T(8,128)S(1)} %get-tuple-element.76, f32[1024,128]{0,1:T(8,128)S(1)} %get-tuple-element.64, f32[1024,128]{0,1:T(8,128)S(1)} %get-tuple-element.63), kind=kOutput, calls=%fused_computation.17 | convolution fusion | flops 805568512 | bytes 2359296 | tf_op jit(solution)/shard_map/transpose(jvp())/dot_general | solution.py:24
  64.1 0.8 add_bitcast_fusion
  64.9 0.0 all-reduce.13.cloned.1.call-update
  65.0 0.6 copy.33
  65.5 0.1 fusion.54
  65.7 1.1 convolution_bitcast_fusion.3
  66.7 6.9 %all-reduce.9 = (f32[1,4,256]{2,1,0:T(4,128)}, f32[1,3,256]{2,0,1:T(1,128)}, f32[1,4]{1,0:T(1,128)}) all-reduce(f32[1,4,256]{2,1,0:T(4,128)S(1)} %convolution_bitcast_fusion.3, f32[1,3,256]{2,0,1:T(1,128)S(1)} %broadcast_in_dim.83, f32[1,4]{1,0:T(1,128)S(1)} %bitcast.151), channel_id=1, replica_groups=mesh['slab'=8,'rays'=4] {'rays'}, use_global_device_ids=true, to_apply=%region_13.15 | all-reduce | flops 1796 | bytes 14368 | tf_op jit(solution)/shard_map/psum | solution.py:78
  73.7 23.7 %all-reduce.13.cloned.1.call-done = (f32[1,256,256]{2,1,0:T(8,128)}, f32[1,2,256,256]{3,2,1,0:T(8,128)}) async-done(((f32[1,256,256]{2,1,0:T(8,128)}, f32[1,2,256,256]{3,2,1,0:T(8,128)}), (f32[1,256,256]{2,1,0:T(8,128)}, f32[1,2,256,256]{3,2,1,0:T(8,128)})) %all-reduce.13.cloned.1.call-update) | async-done | bytes 786448 | tf_op jit(solution)/shard_map/psum | solution.py:78
  97.4 1.7 %copy.76 = f32[1,256,256]{2,1,0:T(8,128)} copy(f32[1,256,256]{2,1,0:T(8,128)} %get-tuple-element.84) | data formatting | bytes 524288
  99.1 0.8 copy.77
  (59 shorter events, 0.5 us)
Async XLA Ops:
  7.2 7.4 %copy-start = (f32[1,256,256]{2,1,0:T(8,128)S(1)}, f32[1,256,256]{2,1,0:T(8,128)}, u32[]{:S(2)}) copy-start(f32[1,256,256]{2,1,0:T(8,128)} %param.15) | copy-start | bytes 786436
  7.2 0.7 copy-start.9
  7.2 0.7 copy-start.2
  7.9 0.7 copy-start.3
  8.7 0.7 copy-start.4
  14.5 1.8 %copy-start.7 = (f32[1,2,256,256]{3,2,1,0:T(8,128)S(1)}, f32[1,2,256,256]{3,2,1,0:T(8,128)}, u32[]{:S(2)}) copy-start(f32[1,2,256,256]{3,2,1,0:T(8,128)} %param.16) | copy-start | bytes 1572868
  17.8 1.5 %copy-start.11 = (f32[1024,256]{1,0:T(8,128)}, f32[1024,256]{1,0:T(8,128)S(1)}, u32[]{:S(2)}) copy-start(f32[1024,256]{1,0:T(8,128)S(1)} %convolution_add_fusion.1) | copy-start | bytes 3145732
  17.9 1.5 %copy-start.8 = (f32[1,4,256]{2,1,0:T(4,128)S(1)}, f32[1,4,256]{2,1,0:T(4,128)}, u32[]{:S(2)}) copy-start(f32[1,4,256]{2,1,0:T(4,128)} %param.17) | copy-start | bytes 12292
  19.3 2.2 %copy-start.13 = (f32[1024,256]{1,0:T(8,128)}, f32[1024,256]{1,0:T(8,128)S(1)}, u32[]{:S(2)}) copy-start(f32[1024,256]{1,0:T(8,128)S(1)} %convolution_add_fusion) | copy-start | bytes 3145732
  19.3 0.7 copy-start.10
  21.6 0.7 copy-start.5
  23.1 14.2 %all-to-all-start = ((f32[4,1,128]{0,1,2:T(1,128)}), f32[4,1,128]{0,1,2:T(1,128)S(1)}, u32[]{:S(2)}, u32[]{:S(2)}) async-start(f32[4,1,128]{0,1,2:T(1,128)} %bitcast.13), calls=%async_computation | async-start | bytes 131072 | tf_op jit(solution)/shard_map/all_to_all | solution.py:69
  39.6 0.7 copy-start.6
  41.2 9.9 %all-to-all-start.1 = ((f32[4,8,16]{2,0,1:T(4,128)}), f32[4,8,16]{2,0,1:T(4,128)S(1)}, u32[]{:S(2)}, u32[]{:S(2)}) async-start(f32[4,8,16]{2,0,1:T(4,128)} %copy.31), calls=%async_computation.1 | async-start | bytes 32768 | tf_op jit(solution)/shard_map/all_to_all | solution.py:74
  44.5 52.9 %all-reduce.13.cloned.1.call-start = ((), (), s32[]{:S(2)}) async-start(), calls=%async_computation.2 | async-start | bytes 1572864 | tf_op jit(solution)/shard_map/psum | solution.py:78
  51.4 3.0 %copy-start.12 = (f32[1024,256]{1,0:T(8,128)S(1)}, f32[1024,256]{1,0:T(8,128)}, u32[]{:S(2)}) copy-start(f32[1024,256]{1,0:T(8,128)} %copy-done.11) | copy-start | bytes 3145732
  64.1 1.6 %copy-start.14 = (f32[1024,256]{1,0:T(8,128)S(1)}, f32[1024,256]{1,0:T(8,128)}, u32[]{:S(2)}) copy-start(f32[1024,256]{1,0:T(8,128)} %copy-done.13) | copy-start | bytes 3145732
  97.4 1.7 %copy-start.1 = (f32[1,2,256,256]{3,2,1,0:T(8,128)S(1)}, f32[1,2,256,256]{3,2,1,0:T(8,128)}, u32[]{:S(2)}) copy-start(f32[1,2,256,256]{3,2,1,0:T(8,128)} %get-tuple-element.85) | copy-start | bytes 1572868
Sparse Core Ops, SparseCore 0:
  65.1 32.2 all-reduce.12
where the time goes:
time: 107 us
  waiting for transfers between devices  36.9 us (34%)
  matrix products  25.1 us (23%)
  between operations  14.4 us (13%)
  local copies, waits for them, and re-layouts  11.1 us (10%)
  starting transfers between devices  10.9 us (10%)
  blocking collectives  6.95 us (6%)
  other arithmetic  1.54 us (1%)
    psum x1, waiting for transfers between devices, shards(): lax.psum((grads[0], grads[1], grads[2], grads[3], grads[4]), 'rays')  23.7 us
    dot_general x8, matrix products, hidden_layer(): return jax.nn.softplus(jnp.dot(hidden, weight, precision=HIGH) + bias)  14.3 us
    all_to_all x1, starting transfers between devices, shards(): lax.all_to_all(seg[:, None, :], 'slab', split_axis=2, concat_axis=1, tile...  7.31 us
    unnamed x36, local copies, waits for them, and re-layouts  7.28 us
    psum x1, blocking collectives, shards(): lax.psum((grads[0], grads[1], grads[2], grads[3], grads[4]), 'rays')  6.95 us
    all_to_all x1, waiting for transfers between devices, shards(): lax.all_to_all(seg[:, None, :], 'slab', split_axis=2, concat_axis=1, tile...  6.88 us
    all_to_all x1, waiting for transfers between devices, shards(): lax.all_to_all(owned_adjoint, 'slab', split_axis=1, concat_axis=2, tiled=...  6.27 us
    dot_general x3, matrix products, head(): jnp.einsum('ch,nh->cn', w_out, hidden, precision=HIGH) + b_out[:, None]  5.6 us
  transfers between devices with their start and end apart: 3, of which 3 were waited for; matrix products, arithmetic and copies ran while one was open for 2% of the time, Pallas kernels for 0%

commit v1 on v0

--- a/solution.py
+++ b/solution.py
@@ -71,9 +71,12 @@
         lambda s: composite(s, local_targets, factor), owned, has_aux=True
     )
     owned_adjoint = pullback(jnp.ones((), jnp.float32))[0]
-    adjoint = lax.all_to_all(owned_adjoint, "slab", split_axis=1, concat_axis=2, tiled=True)[
-        :, 0, :
-    ]
+    adjoint = jnp.concatenate(
+        lax.all_to_all(
+            jnp.stack(jnp.split(owned_adjoint, lax.axis_size("slab"), axis=1)), "slab", 0, 0
+        ),
+        axis=2,
+    )[:, 0, :]
     grads = pull_all(adjoint)[0]
     grad_in, grad_mid, grad_out, grad_hid, grad_bout = lax.psum(
         (grads[0], grads[1], grads[2], grads[3], grads[4]), "rays"

time: 107 us -> 111 us (1.037)
  local copies, waits for them, and re-layouts: 11.1 us -> 15.1 us
    unnamed x36 -> x43, local copies, waits for them, and re-layouts: 7.28 us -> 11.3 us
where the time goes in v1:
time: 111 us
  waiting for transfers between devices  36.9 us (33%)
  matrix products  25.1 us (23%)
  local copies, waits for them, and re-layouts  15.1 us (14%)
  between operations  14.4 us (13%)
  starting transfers between devices  10.9 us (10%)
  blocking collectives  6.94 us (6%)
  other arithmetic  1.55 us (1%)
    psum x1, waiting for transfers between devices, shards(): lax.psum((grads[0], grads[1], grads[2], grads[3], grads[4]), 'rays')  23.7 us
    dot_general x8, matrix products, hidden_layer(): return jax.nn.softplus(jnp.dot(hidden, weight, precision=HIGH) + bias)  14.4 us
    unnamed x43, local copies, waits for them, and re-layouts  11.3 us
    all_to_all x1, starting transfers between devices, shards(): lax.all_to_all(seg[:, None, :], 'slab', split_axis=2, concat_axis=1, tile...  7.31 us
    psum x1, blocking collectives, shards(): lax.psum((grads[0], grads[1], grads[2], grads[3], grads[4]), 'rays')  6.94 us
    all_to_all x1, waiting for transfers between devices, shards(): lax.all_to_all(seg[:, None, :], 'slab', split_axis=2, concat_axis=1, tile...  6.88 us
    all_to_all x1, waiting for transfers between devices, shards(): lax.all_to_all(jnp.stack(jnp.split(owned_adjoint, lax.axis_size('slab'),...  6.27 us
    dot_general x3, matrix products, head(): jnp.einsum('ch,nh->cn', w_out, hidden, precision=HIGH) + b_out[:, None]  5.6 us
  transfers between devices with their start and end apart: 3, of which 3 were waited for; matrix products, arithmetic and copies ran while one was open for 2% of the time, Pallas kernels for 0%

profile of v1, /device:TPU:0, one launch (start us, length us, event | category | flops | bytes accessed | tf_op | source)
XLA Modules:
  0.0 110.8 jit_solution(17583533350170487881)
XLA Ops:
  7.2 0.7 copy-done.9
  7.9 0.7 copy-done.3
  8.7 0.7 copy-done.4
  9.4 5.2 %fusion.76 = (f32[1024,128]{0,1:T(8,128)S(1)}, f32[1024,128]{0,1:T(8,128)S(1)}) fusion(f32[1,3,128]{2,0,1:T(1,128)S(1)} %copy-done.4, f32[1,3,8,128]{3,2,1,0:T(8,128)S(1)} %add_bitcast_fusion.1), kind=kOutput, calls=%fused_computation.158 | convolution fusion | flops 4718592 | bytes 1062400 | tf_op jit(solution)/shard_map/dk,dn->nk/dot_general | solution.py:19
  14.6 1.8 %convolution_add_fusion.2 = f32[1024,256]{1,0:T(8,128)S(1)} fusion(f32[1024,128]{0,1:T(8,128)S(1)} %get-tuple-element.64, f32[1024,128]{0,1:T(8,128)S(1)} %get-tuple-element.63, f32[256]{0:T(256)S(1)} %bitcast.169, f32[1,256,256]{2,1,0:T(8,128)S(1)} %copy-done), kind=kOutput, calls=%fused_computation.14 | convolution fusion | flops 805830656 | bytes 2360320 | tf_op jit(solution)/shard_map/jvp()/dot_general | solution.py:24
  16.4 1.4 %convolution_add_fusion.1 = f32[1024,256]{1,0:T(8,128)S(1)} fusion(f32[1024,256]{1,0:T(8,128)S(1)} %convolution_add_fusion.2, f32[256]{0:T(256)S(1)} %bitcast.178, f32[1,2,256,256]{3,2,1,0:T(8,128)S(1)} %copy-done.7), kind=kOutput, calls=%fused_computation.13 | convolution fusion | flops 807141376 | bytes 2360320 | tf_op jit(solution)/shard_map/jvp()/dot_general | solution.py:24
  17.9 1.5 %convolution_add_fusion = f32[1024,256]{1,0:T(8,128)S(1)} fusion(f32[1024,256]{1,0:T(8,128)S(1)} %convolution_add_fusion.1, f32[256]{0:T(256)S(1)} %bitcast.177, f32[1,2,256,256]{3,2,1,0:T(8,128)S(1)} %copy-done.7), kind=kOutput, calls=%fused_computation.12 | convolution fusion | flops 807141376 | bytes 2360320 | tf_op jit(solution)/shard_map/jvp()/dot_general | solution.py:24
  19.4 0.7 copy-done.10
  20.0 1.5 %fusion = f32[4,1024]{1,0:T(4,128)S(1)} fusion(f32[1024,256]{1,0:T(8,128)S(1)} %convolution_add_fusion, f32[4]{0:T(128)S(1)} %bitcast.179, f32[1,4,256]{2,1,0:T(4,128)S(1)} %copy-done.8), kind=kOutput, calls=%fused_computation.19 | convolution fusion | flops 14159872 | bytes 1069072 | tf_op jit(solution)/shard_map/jvp(ch,nh->cn)/dot_general | solution.py:30
  21.6 0.6 copy-done.5
  22.4 0.8 copy.30
  23.1 7.3 %all-to-all-start = ((f32[4,1,128]{0,1,2:T(1,128)}), f32[4,1,128]{0,1,2:T(1,128)S(1)}, u32[]{:S(2)}, u32[]{:S(2)}) async-start(f32[4,1,128]{0,1,2:T(1,128)} %bitcast.13), calls=%async_computation | async-start | bytes 131072 | tf_op jit(solution)/shard_map/all_to_all | solution.py:69
  30.5 6.9 %all-to-all-done = f32[4,1,128]{0,1,2:T(1,128)S(1)} async-done(((f32[4,1,128]{0,1,2:T(1,128)}), f32[4,1,128]{0,1,2:T(1,128)S(1)}, u32[]{:S(2)}, u32[]{:S(2)}) %all-to-all-start) | async-done | bytes 2080 | tf_op jit(solution)/shard_map/all_to_all | solution.py:69
  37.3 1.8 %slice_reduce_fusion = f32[128]{0:T(128)S(1)} fusion(f32[4,1,128]{0,1,2:T(1,128)S(1)} %all-to-all-done), kind=kLoop, calls=%fused_computation.44 | loop fusion | bytes 1024 | tf_op jit(solution)/shard_map/jvp()/slice | solution.py:50
  39.2 0.1 squeeze.38
  39.3 0.1 squeeze.41
  39.3 0.1 copy.38
  39.5 0.1 slice.58
  39.6 0.7 copy-done.6
  40.3 0.1 broadcast_in_dim.73
  40.4 0.1 reshape.384
  40.6 0.6 constant_dynamic-update-slice_fusion.7
  41.2 0.6 constant_dynamic-update-slice_fusion.6
  41.8 0.6 constant_dynamic-update-slice_fusion.5
  42.3 0.6 constant_dynamic-update-slice_fusion.4
  42.9 0.6 constant_dynamic-update-slice_fusion.3
  43.5 0.6 constant_dynamic-update-slice_fusion.2
  44.1 0.6 constant_dynamic-update-slice_fusion.1
  44.6 0.6 constant_dynamic-update-slice_fusion
  45.2 3.3 %all-to-all-start.1 = ((f32[8,4,1,16]{3,1,2,0:T(4,128)}), f32[8,4,1,16]{3,1,2,0:T(4,128)S(1)}, u32[]{:S(2)}, u32[]{:S(2)}) async-start(f32[8,4,1,16]{3,1,2,0:T(4,128)} %constant_dynamic-update-slice_fusion), calls=%async_computation.1 | async-start | bytes 32768 | tf_op jit(solution)/shard_map/all_to_all | solution.py:75
  48.6 0.2 all-reduce.13.cloned.1.call-start
  48.8 6.3 %all-to-all-done.1 = f32[8,4,1,16]{3,1,2,0:T(4,128)S(1)} async-done(((f32[8,4,1,16]{3,1,2,0:T(4,128)}), f32[8,4,1,16]{3,1,2,0:T(4,128)S(1)}, u32[]{:S(2)}, u32[]{:S(2)}) %all-to-all-start.1) | async-done | bytes 2080 | tf_op jit(solution)/shard_map/all_to_all | solution.py:75
  55.1 0.1 neg.109
  55.2 0.1 split.41
  55.5 3.0 %fusion.82 = (f32[256]{0:T(256)S(1)}, f32[1024,256]{1,0:T(8,128)S(1)}) fusion(f32[1024,256]{1,0:T(8,128)} %copy-done.13, f32[1,4,256]{2,1,0:T(4,128)S(1)} %copy-done.8, f32[1,1024]{1,0:T(1,128)S(1)} %fusion.36, f32[3,1024]{1,0:T(4,128)S(1)} %get-tuple-element.65), kind=kOutput, calls=%fused_computation.164 | convolution fusion | flops 15994624 | bytes 2118656 | tf_op jit(solution)/shard_map/transpose(jvp(ch,nh->cn))/dot_general | solution.py:30
  58.5 2.3 %convolution_bitcast_fusion.1 = f32[1,256,256]{2,1,0:T(8,128)S(1)} fusion(f32[1024,256]{1,0:T(8,128)S(1)} %get-tuple-element.88, f32[1024,256]{1,0:T(8,128)S(1)} %copy-done.12), kind=kOutput, calls=%fused_computation.16 | convolution fusion | flops 806879232 | bytes 2359296 | tf_op jit(solution)/shard_map/transpose(jvp())/dot_general | solution.py:24
  60.8 1.7 %fusion.81 = (f32[256]{0:T(256)S(1)}, f32[1024,256]{1,0:T(8,128)S(1)}) fusion(f32[1024,256]{1,0:T(8,128)S(1)} %copy-done.12, f32[1024,256]{1,0:T(8,128)S(1)} %get-tuple-element.88, f32[1,2,256,256]{3,2,1,0:T(8,128)S(1)} %copy-done.7), kind=kOutput, calls=%fused_computation.163 | convolution fusion | flops 808713984 | bytes 3408896 | tf_op jit(solution)/shard_map/transpose(jvp())/dot_general | solution.py:24
  62.5 2.3 %convolution_bitcast_fusion = f32[1,256,256]{2,1,0:T(8,128)S(1)} fusion(f32[1024,256]{1,0:T(8,128)S(1)} %get-tuple-element.86, f32[1024,256]{1,0:T(8,128)S(1)} %convolution_add_fusion.2), kind=kOutput, calls=%fused_computation.15 | convolution fusion | flops 806879232 | bytes 2359296 | tf_op jit(solution)/shard_map/transpose(jvp())/dot_general | solution.py:24
  64.7 1.7 %fusion.80 = (f32[256]{0:T(256)S(1)}, f32[1024,256]{1,0:T(8,128)S(1)}) fusion(f32[1024,256]{1,0:T(8,128)S(1)} %convolution_add_fusion.2, f32[1024,256]{1,0:T(8,128)S(1)} %get-tuple-element.86, f32[1,2,256,256]{3,2,1,0:T(8,128)S(1)} %copy-done.7), kind=kOutput, calls=%fused_computation.162 | convolution fusion | flops 808713984 | bytes 3408896 | tf_op jit(solution)/shard_map/transpose(jvp())/dot_general | solution.py:24
  66.4 1.7 %convolution_bitcast_fusion.2 = f32[1,256,256]{2,1,0:T(8,128)} fusion(f32[1024,256]{1,0:T(8,128)S(1)} %get-tuple-element.84, f32[1024,128]{0,1:T(8,128)S(1)} %get-tuple-element.64, f32[1024,128]{0,1:T(8,128)S(1)} %get-tuple-element.63), kind=kOutput, calls=%fused_computation.17 | convolution fusion | flops 805568512 | bytes 2359296 | tf_op jit(solution)/shard_map/transpose(jvp())/dot_general | solution.py:24
  68.2 0.8 add_bitcast_fusion
  69.0 0.6 copy.33
  69.6 0.1 fusion.61
  69.7 1.1 convolution_bitcast_fusion.3
  70.8 6.9 %all-reduce.9 = (f32[1,4,256]{2,1,0:T(4,128)}, f32[1,3,256]{2,0,1:T(1,128)}, f32[1,4]{1,0:T(1,128)}) all-reduce(f32[1,4,256]{2,1,0:T(4,128)S(1)} %convolution_bitcast_fusion.3, f32[1,3,256]{2,0,1:T(1,128)S(1)} %broadcast_in_dim.83, f32[1,4]{1,0:T(1,128)S(1)} %bitcast.173), channel_id=1, replica_groups=mesh['slab'=8,'rays'=4] {'rays'}, use_global_device_ids=true, to_apply=%region_13.15 | all-reduce | flops 1796 | bytes 14368 | tf_op jit(solution)/shard_map/psum | solution.py:81
  77.7 23.7 %all-reduce.13.cloned.1.call-done = (f32[1,256,256]{2,1,0:T(8,128)}, f32[1,2,256,256]{3,2,1,0:T(8,128)}) async-done(((f32[1,256,256]{2,1,0:T(8,128)}, f32[1,2,256,256]{3,2,1,0:T(8,128)}), (f32[1,256,256]{2,1,0:T(8,128)}, f32[1,2,256,256]{3,2,1,0:T(8,128)})) %all-reduce.13.cloned.1.call-update) | async-done | bytes 786448 | tf_op jit(solution)/shard_map/psum | solution.py:81
  101.5 1.7 %copy.83 = f32[1,256,256]{2,1,0:T(8,128)} copy(f32[1,256,256]{2,1,0:T(8,128)} %get-tuple-element.92) | data formatting | bytes 524288
  103.2 0.8 copy.84
  (66 shorter events, 0.8 us)
Async XLA Ops:
  7.2 7.4 %copy-start = (f32[1,256,256]{2,1,0:T(8,128)S(1)}, f32[1,256,256]{2,1,0:T(8,128)}, u32[]{:S(2)}) copy-start(f32[1,256,256]{2,1,0:T(8,128)} %param.15) | copy-start | bytes 786436
  7.2 0.7 copy-start.9
  7.2 0.7 copy-start.2
  7.9 0.7 copy-start.3
  8.7 0.7 copy-start.4
  14.5 1.8 %copy-start.7 = (f32[1,2,256,256]{3,2,1,0:T(8,128)S(1)}, f32[1,2,256,256]{3,2,1,0:T(8,128)}, u32[]{:S(2)}) copy-start(f32[1,2,256,256]{3,2,1,0:T(8,128)} %param.16) | copy-start | bytes 1572868
  17.8 1.5 %copy-start.11 = (f32[1024,256]{1,0:T(8,128)}, f32[1024,256]{1,0:T(8,128)S(1)}, u32[]{:S(2)}) copy-start(f32[1024,256]{1,0:T(8,128)S(1)} %convolution_add_fusion.1) | copy-start | bytes 3145732
  17.9 1.5 %copy-start.8 = (f32[1,4,256]{2,1,0:T(4,128)S(1)}, f32[1,4,256]{2,1,0:T(4,128)}, u32[]{:S(2)}) copy-start(f32[1,4,256]{2,1,0:T(4,128)} %param.17) | copy-start | bytes 12292
  19.3 2.2 %copy-start.13 = (f32[1024,256]{1,0:T(8,128)}, f32[1024,256]{1,0:T(8,128)S(1)}, u32[]{:S(2)}) copy-start(f32[1024,256]{1,0:T(8,128)S(1)} %convolution_add_fusion) | copy-start | bytes 3145732
  19.4 0.7 copy-start.10
  21.6 0.7 copy-start.5
  23.1 14.2 %all-to-all-start = ((f32[4,1,128]{0,1,2:T(1,128)}), f32[4,1,128]{0,1,2:T(1,128)S(1)}, u32[]{:S(2)}, u32[]{:S(2)}) async-start(f32[4,1,128]{0,1,2:T(1,128)} %bitcast.13), calls=%async_computation | async-start | bytes 131072 | tf_op jit(solution)/shard_map/all_to_all | solution.py:69
  39.6 0.7 copy-start.6
  45.2 9.9 %all-to-all-start.1 = ((f32[8,4,1,16]{3,1,2,0:T(4,128)}), f32[8,4,1,16]{3,1,2,0:T(4,128)S(1)}, u32[]{:S(2)}, u32[]{:S(2)}) async-start(f32[8,4,1,16]{3,1,2,0:T(4,128)} %constant_dynamic-update-slice_fusion), calls=%async_computation.1 | async-start | bytes 32768 | tf_op jit(solution)/shard_map/all_to_all | solution.py:75
  48.6 52.9 %all-reduce.13.cloned.1.call-start = ((), (), s32[]{:S(2)}) async-start(), calls=%async_computation.2 | async-start | bytes 1572864 | tf_op jit(solution)/shard_map/psum | solution.py:81
  55.4 3.1 %copy-start.12 = (f32[1024,256]{1,0:T(8,128)S(1)}, f32[1024,256]{1,0:T(8,128)}, u32[]{:S(2)}) copy-start(f32[1024,256]{1,0:T(8,128)} %copy-done.11) | copy-start | bytes 3145732
  68.2 1.6 %copy-start.14 = (f32[1024,256]{1,0:T(8,128)S(1)}, f32[1024,256]{1,0:T(8,128)}, u32[]{:S(2)}) copy-start(f32[1024,256]{1,0:T(8,128)} %copy-done.13) | copy-start | bytes 3145732
  101.5 1.7 %copy-start.1 = (f32[1,2,256,256]{3,2,1,0:T(8,128)S(1)}, f32[1,2,256,256]{3,2,1,0:T(8,128)}, u32[]{:S(2)}) copy-start(f32[1,2,256,256]{3,2,1,0:T(8,128)} %get-tuple-element.93) | copy-start | bytes 1572868
Sparse Core Ops, SparseCore 0:
  69.1 32.2 all-reduce.12
